TPU v7x, 256 devices: a whole 4x4x8 slice. The times are simulated.
256 devices in a mesh: seq: 32 (over y_lo, z, core), tp: 8 (over x, y_hi).
Axes of the slice: x: 4, y: 4 (y_hi: 2, y_lo: 2; y = y_hi * 2 + y_lo), z: 8, core: 2. Of those that a mesh axis runs over, the one named last changes fastest.
Arguments:
- hidden: bfloat16 [8192, 4096], P('seq', 'tp'), may hold values from -6 to 6
- neighbours: bfloat16 [128, 256, 896], P('seq'), may hold values from -6 to 6
- enc_gain: float32 [896], replicated, may hold values from 0.25 to 1.75
- enc_w1: bfloat16 [896, 3584], P(None, 'tp'), may hold values from -0.1875 to 0.1875
- enc_w2: bfloat16 [3584, 896], P('tp'), may hold values from -0.09375 to 0.09375
- key_weight: bfloat16 [896, 4096], P(None, 'tp'), may hold values from -0.1875 to 0.1875
- value_weight: bfloat16 [896, 4096], P(None, 'tp'), may hold values from -0.1875 to 0.1875
- dec_gain: float32 [4096], replicated, may hold values from 0.25 to 1.75
- query_weight: bfloat16 [4096, 4096], P('seq', 'tp'), may hold values from -0.09375 to 0.09375
- out_weight: bfloat16 [4096, 4096], P('tp', 'seq'), may hold values from -0.09375 to 0.09375
Outputs:
- mixed: bfloat16 [8192, 4096], P('seq', 'tp')
All inputs are finite; a program needn't handle non-finite values.
Results may differ from a plain program's by a relative error of at most 0.015.
Values may be sent and summed in bfloat16 or wider, within the bound.
A program may use at most 64 MiB of HBM per device.

v0:
```python
import jax
import jax.numpy as jnp
from jax import lax
from jax.sharding import PartitionSpec as P

HD = 128
M = 64
NEIGH = 2
RLEN = 128


def copy_for_each(value, axis):
    copies = jnp.broadcast_to(value, (lax.axis_size(axis), *value.shape))
    return lax.all_to_all(copies, axis, split_axis=0, concat_axis=0, tiled=True)


def in_order(tiles, dim):
    tiles = jnp.moveaxis(tiles, 0, dim)
    shape = tiles.shape
    return tiles.reshape(*shape[:dim], shape[dim] * shape[dim + 1], *shape[dim + 2 :])


def collect(value, axis, dim):
    tiles = copy_for_each(value, axis)
    return in_order(tiles, dim)


def shifted(value, axis, by):
    devices = lax.axis_size(axis)
    pairs = [(i, i + by) for i in range(devices) if 0 <= i + by < devices]
    return lax.ppermute(value, axis, pairs)


def in_blocks(value, dim, devices):
    shape = value.shape
    tiles = value.reshape(*shape[:dim], devices, shape[dim] // devices, *shape[dim + 1 :])
    return jnp.moveaxis(tiles, dim, 0)


def summed_on_arrival(value, axis, dim):
    devices = lax.axis_size(axis)
    tiles = lax.all_to_all(in_blocks(value, dim, devices), axis, 0, 0, tiled=True)
    return jnp.sum(tiles.astype(jnp.float32), axis=0)


def rms_scale(values32, gain):
    return (
        values32 * lax.rsqrt(jnp.mean(values32 * values32, axis=-1, keepdims=True) + 1e-06) * gain
    )


def feed_partial(tokens, enc_gain, first_weight, second_weight):
    enc_norm = rms_scale(tokens.astype(jnp.float32), enc_gain).astype(jnp.bfloat16)
    inner = jax.nn.relu(jnp.dot(enc_norm, first_weight, preferred_element_type=jnp.float32)).astype(
        jnp.bfloat16
    )
    return jnp.dot(inner, second_weight, preferred_element_type=jnp.float32)


def encode(batch, enc_gain, enc_w1, enc_w2):
    row_count = batch.shape[0] * batch.shape[1]
    flat = batch.reshape(row_count, batch.shape[2])
    share = row_count // lax.axis_size("tp")
    portion = lax.psum_scatter(
        feed_partial(flat, enc_gain, enc_w1, enc_w2).astype(jnp.bfloat16),
        "tp",
        scatter_dimension=0,
        tiled=True,
    ).astype(jnp.float32)
    mine = lax.dynamic_slice_in_dim(flat, lax.axis_index("tp") * share, share, 0)
    result = (mine.astype(jnp.float32) + portion).astype(jnp.bfloat16)
    return collect(result, "tp", 0)


def project_heads(encoded, weight, span_count):
    result = jnp.dot(encoded, weight, preferred_element_type=jnp.float32).astype(jnp.bfloat16)
    return result.reshape(span_count, NEIGH * RLEN, weight.shape[1] // HD, HD)


def per_device(
    hidden,
    neighbours,
    enc_gain,
    enc_w1,
    enc_w2,
    key_weight,
    value_weight,
    dec_gain,
    query_weight,
    out_weight,
):
    tok_rows = hidden.shape[0]
    span_count = neighbours.shape[0]
    encoded = encode(neighbours, enc_gain, enc_w1, enc_w2)
    keys_here = project_heads(encoded, key_weight, span_count)
    values_here = project_heads(encoded, value_weight, span_count)
    stacked = jnp.stack([keys_here[span_count - 1], values_here[span_count - 1]])
    earlier = shifted(stacked, "seq", 1)
    keys_all = jnp.concatenate([earlier[0:1], keys_here], axis=0)
    values_all = jnp.concatenate([earlier[1:2], values_here], axis=0)
    features = collect(hidden, "tp", 1)
    dec_norm = rms_scale(features.astype(jnp.float32), dec_gain).astype(jnp.bfloat16)
    query = jnp.dot(
        dec_norm,
        lax.all_gather(query_weight, "seq", axis=0, tiled=True),
        preferred_element_type=jnp.float32,
    ).astype(jnp.bfloat16)
    head_count = query.shape[1] // HD
    grouped = jnp.pad(query, ((1, M - 1), (0, 0))).reshape(span_count + 1, M, head_count, HD)
    scores = jnp.einsum(
        "cmhd,cnhd->chmn", grouped, keys_all, preferred_element_type=jnp.float32
    ) * HD ** (-0.5)
    probs = jax.nn.softmax(scores, axis=-1).astype(jnp.bfloat16)
    attn = jnp.einsum(
        "chmn,cnhd->cmhd", probs, values_all, preferred_element_type=jnp.float32
    ).astype(jnp.bfloat16)
    attn = attn.reshape((span_count + 1) * M, head_count * HD)[1 : tok_rows + 1]
    position = lax.axis_index("seq") * tok_rows + jnp.arange(tok_rows, dtype=jnp.int32)[:, None]
    attn = jnp.where(position >= M - 1, attn, jnp.zeros_like(attn))
    partial_value = jnp.dot(
        attn,
        lax.all_gather(out_weight, "seq", axis=1, tiled=True),
        preferred_element_type=jnp.float32,
    )
    branch = summed_on_arrival(partial_value.astype(jnp.bfloat16), "tp", 1)
    return (hidden.astype(jnp.float32) + branch).astype(jnp.bfloat16)


def solution(mesh):
    placed = (
        P("seq", "tp"),
        P("seq", None, None),
        P(),
        P(None, "tp"),
        P("tp", None),
        P(None, "tp"),
        P(None, "tp"),
        P(),
        P("seq", "tp"),
        P("tp", "seq"),
    )
    return jax.shard_map(
        per_device, mesh=mesh, in_specs=placed, out_specs=P("seq", "tp"), check_vma=False
    )
```

profile of v0, /device:TPU:8, one launch (start us, length us, event | category | flops | bytes accessed | tf_op | source)
XLA Modules:
  0.0 238.6 jit_solution(4161549180704178603)
XLA Ops:
  7.4 2.0 multiply_reduce_fusion.1
  9.4 5.5 %convolution_convert_fusion.1 = bf16[1024,896]{1,0:T(8,128)(2,1)} fusion(bf16[448,896]{1,0:T(8,128)(2,1)} %param.14, bf16[896,448]{0,1:T(8,128)(2,1)} %param.13, bf16[1024,896]{1,0:T(8,128)(2,1)} %bitcast.43, f32[896]{0:T(1024)} %param.12, f32[1024]{0:T(1024)S(1)} %bitcast.50), kind=kOutput, calls=%fused_computation.14 | convolution fusion | flops 1649672192 | bytes 5283328 | tf_op jit(solution)/shard_map/dot_general | solution.py:57
  16.3 1.5 broadcast_in_dim.26
  17.8 6.0 %all-to-all-start.1 = ((bf16[8,256,512]{1,2,0:T(8,128)(2,1)}), bf16[8,256,512]{1,2,0:T(8,128)(2,1)S(1)}, u32[]{:S(2)}, u32[]{:S(2)}) async-start(bf16[8,256,512]{1,2,0:T(8,128)(2,1)} %broadcast_in_dim.26), calls=%async_computation.2 | async-start | bytes 4194304 | tf_op jit(solution)/shard_map/all_to_all | solution.py:14
  23.8 90.0 %reduce-scatter.2.cloned.1.call-done = bf16[128,896]{1,0:T(8,128)(2,1)} async-done(((bf16[1024,896]{1,0:T(8,128)(2,1)}), bf16[128,896]{1,0:T(8,128)(2,1)}) %reduce-scatter.2.cloned.1.call-update) | async-done | bytes 229392 | tf_op jit(solution)/shard_map/reduce_scatter | solution.py:64
  114.9 1.5 broadcast_in_dim.12
  116.4 4.4 %all-to-all-start = ((bf16[8,128,896]{2,1,0:T(8,128)(2,1)}), bf16[8,128,896]{2,1,0:T(8,128)(2,1)}, u32[]{:S(2)}, u32[]{:S(2)}) async-start(bf16[8,128,896]{2,1,0:T(8,128)(2,1)} %broadcast_in_dim.12), calls=%async_computation.1 | async-start | bytes 3670016 | tf_op jit(solution)/shard_map/all_to_all | solution.py:14
  122.4 24.0 %all-to-all-done = bf16[8,128,896]{2,1,0:T(8,128)(2,1)} async-done(((bf16[8,128,896]{2,1,0:T(8,128)(2,1)}), bf16[8,128,896]{2,1,0:T(8,128)(2,1)}, u32[]{:S(2)}, u32[]{:S(2)}) %all-to-all-start) | async-done | bytes 1835040 | tf_op jit(solution)/shard_map/all_to_all | solution.py:14
  146.5 2.8 %convolution_convert_fusion.3 = bf16[1024,512]{0,1:T(8,128)(2,1)S(1)} fusion(bf16[1024,896]{1,0:T(8,128)(2,1)} %bitcast.1, bf16[896,512]{1,0:T(8,128)(2,1)S(1)} %copy-done), kind=kOutput, calls=%fused_computation.17 | convolution fusion | flops 940048384 | bytes 3801088 | tf_op jit(solution)/shard_map/dot_general | solution.py:76
  150.4 3.0 %convolution_convert_fusion.2 = bf16[1024,512]{0,1:T(8,128)(2,1)S(1)} fusion(bf16[1024,896]{1,0:T(8,128)(2,1)} %bitcast.1, bf16[896,512]{1,0:T(8,128)(2,1)} %param.16), kind=kOutput, calls=%fused_computation.16 | convolution fusion | flops 940048384 | bytes 3801088 | tf_op jit(solution)/shard_map/dot_general | solution.py:76
  155.4 1.8 pad_maximum_fusion
  157.2 2.1 collective-permute-start
  159.3 2.3 fusion.2
  161.7 1.9 reshape.66
  163.5 1.9 reshape.64
  165.4 1.5 copy.27
  166.9 1.5 copy.25
  168.3 1.8 collective-permute-done
  171.0 4.2 %convolution_convert_fusion.4 = bf16[256,512]{1,0:T(8,128)(2,1)S(1)} fusion(bf16[256,4096]{0,1:T(8,128)(2,1)} %fusion.2, bf16[4096,512]{1,0:T(8,128)(2,1)} %all-gather.3.cloned.1.call-done), kind=kOutput, calls=%fused_computation.29 | convolution fusion | flops 1073872896 | bytes 6553600 | tf_op jit(solution)/shard_map/dot_general | solution.py:103
  176.1 2.9 %fusion.42 = (f32[5,4,64]{2,1,0:T(4,128)S(1)}, f32[5,4,64,256]{3,2,1,0:T(8,128)}) fusion(bf16[4,256,4,128]{3,1,2,0:T(8,128)(2,1)S(1)} %copy-done.4, bf16[1,256,4,128]{3,1,2,0:T(8,128)(2,1)} %get-tuple-element.5, bf16[5,64,4,128]{3,2,1,0:T(4,128)(2,1)} %reshape.65), kind=kOutput, calls=%fused_computation.51 | convolution fusion | flops 85524736 | bytes 2954240 | tf_op jit(solution)/shard_map/sub | solution.py:113
  179.0 1.7 fusion.18
  181.0 10.2 %all-gather.5.cloned.1.call-done = bf16[512,4096]{1,0:T(8,128)(2,1)} async-done(((bf16[512,128]{1,0:T(8,128)(2,1)}), bf16[512,4096]{1,0:T(8,128)(2,1)}) %all-gather.5.cloned.1.call-update) | async-done | bytes 4194320 | tf_op jit(solution)/shard_map/all_gather | solution.py:122
  191.3 3.5 %convolution_convert_fusion = bf16[256,4096]{1,0:T(8,128)(2,1)S(1)} fusion(bf16[512,4096]{1,0:T(8,128)(2,1)} %all-gather.5.cloned.1.call-done, bf16[320,512]{1,0:T(8,128)(2,1)S(1)} %bitcast.49, pred[256]{0:T(512)(128)(4,1)S(1)} %copy-done.9), kind=kOutput, calls=%fused_computation.1 | convolution fusion | flops 1074921472 | bytes 6554112 | tf_op jit(solution)/shard_map/dot_general | solution.py:120
  195.0 34.5 %all_to_all.15 = bf16[8,256,512]{2,1,0:T(8,128)(2,1)S(1)} all-to-all(bf16[8,256,512]{2,1,0:T(8,128)(2,1)S(1)} %bitcast.42), channel_id=1, replica_groups=mesh['seq'=32,'tp'=8] {'tp'}, dimensions={0} | all-to-all | bytes 4194304 | tf_op jit(solution)/shard_map/all_to_all | solution.py:42
  (47 shorter events, 11.1 us)
Async XLA Ops:
  7.4 139.1 %copy-start = (bf16[896,512]{1,0:T(8,128)(2,1)S(1)}, bf16[896,512]{1,0:T(8,128)(2,1)}, u32[]{:S(2)}) copy-start(bf16[896,512]{1,0:T(8,128)(2,1)} %param.15) | copy-start | bytes 2752516
  7.4 106.4 %reduce-scatter.2.cloned.1.call-start = ((), (), s32[]{:S(2)}) async-start(), calls=%async_computation.4 | async-start | bytes 2064384 | tf_op jit(solution)/shard_map/reduce_scatter | solution.py:64
  14.9 1.2 copy-start.5
  14.9 156.0 %all-gather.3.cloned.1.call-start = ((), (), s32[]{:S(2)}) async-start(), calls=%async_computation.5 | async-start | bytes 4325376 | tf_op jit(solution)/shard_map/all_gather | solution.py:105
  15.5 175.8 %all-gather.5.cloned.1.call-start = ((), (), s32[]{:S(2)}) async-start(), calls=%async_computation.6 | async-start | bytes 4325376 | tf_op jit(solution)/shard_map/all_gather | solution.py:122
  17.8 97.2 %all-to-all-start.1 = ((bf16[8,256,512]{1,2,0:T(8,128)(2,1)}), bf16[8,256,512]{1,2,0:T(8,128)(2,1)S(1)}, u32[]{:S(2)}, u32[]{:S(2)}) async-start(bf16[8,256,512]{1,2,0:T(8,128)(2,1)} %broadcast_in_dim.26), calls=%async_computation.2 | async-start | bytes 4194304 | tf_op jit(solution)/shard_map/all_to_all | solution.py:14
  116.4 30.1 %all-to-all-start = ((bf16[8,128,896]{2,1,0:T(8,128)(2,1)}), bf16[8,128,896]{2,1,0:T(8,128)(2,1)}, u32[]{:S(2)}, u32[]{:S(2)}) async-start(bf16[8,128,896]{2,1,0:T(8,128)(2,1)} %broadcast_in_dim.12), calls=%async_computation.1 | async-start | bytes 3670016 | tf_op jit(solution)/shard_map/all_to_all | solution.py:14
  149.2 1.0 copy-start.1
  153.5 1.0 copy-start.2
  154.5 4.8 %copy-start.8 = (f32[4096]{0:T(1024)S(1)}, f32[4096]{0:T(1024)}, u32[]{:S(2)}) copy-start(f32[4096]{0:T(1024)} %param.17) | copy-start | bytes 49156
  157.2 12.9 %collective-permute-start = (bf16[2,256,4,128]{3,1,2,0:T(8,128)(2,1)}, bf16[2,256,4,128]{3,1,2,0:T(8,128)(2,1)S(1)}, u32[]{:S(2)}, u32[]{:S(2)}) collective-permute-start(bf16[2,256,4,128]{3,1,2,0:T(8,128)(2,1)} %pad_maximum_fusion), channel_id=1, source_target_pairs={{0,8},{8,16},{16,24},{24,32},{32,40},{40,48},{48,56},{56,64},{64,7... | collective-permute-start | bytes 1572872 | tf_op jit(solution)/shard_map/ppermute | solution.py:31
  170.9 5.1 %copy-start.4 = (bf16[4,256,4,128]{3,1,2,0:T(8,128)(2,1)S(1)}, bf16[4,256,4,128]{3,1,2,0:T(8,128)(2,1)}, u32[]{:S(2)}) copy-start(bf16[4,256,4,128]{3,1,2,0:T(8,128)(2,1)} %copy.27) | copy-start | bytes 3145732
  175.2 3.7 %copy-start.3 = (bf16[4,256,4,128]{3,1,2,0:T(8,128)(2,1)S(1)}, bf16[4,256,4,128]{3,1,2,0:T(8,128)(2,1)}, u32[]{:S(2)}) copy-start(bf16[4,256,4,128]{3,1,2,0:T(8,128)(2,1)} %copy.25) | copy-start | bytes 3145732
  176.1 2.9 %copy-start.7 = (bf16[1,256,4,128]{3,1,2,0:T(8,128)(2,1)S(1)}, bf16[1,256,4,128]{3,1,2,0:T(8,128)(2,1)}, u32[]{:S(2)}) copy-start(bf16[1,256,4,128]{3,1,2,0:T(8,128)(2,1)} %get-tuple-element.6) | copy-start | bytes 786436
  179.0 12.3 %copy-start.9 = (pred[256]{0:T(512)(128)(4,1)S(1)}, pred[256]{0:T(512)(128)(4,1)}, u32[]{:S(2)}) copy-start(pred[256]{0:T(512)(128)(4,1)} %add_compare_fusion) | copy-start | bytes 772
  229.4 1.0 copy-start.6
Sparse Core Ops, SparseCore 0:
  15.1 98.7 reduce-scatter.1
Sparse Core Ops, SparseCore 1:
  17.3 83.1 all-gather.2
  102.1 89.2 all-gather.4
where the time goes:
time: 239 us
  waiting for transfers between devices  127 us (53%)
  blocking collectives  34.5 us (14%)
  matrix products  23.6 us (10%)
  local copies, waits for them, and re-layouts  15.7 us (7%)
  between operations  15 us (6%)
  starting transfers between devices  12.6 us (5%)
  other arithmetic  10.1 us (4%)
    reduce_scatter x1, waiting for transfers between devices, encode(): lax.psum_scatter(feed_partial(flat, enc_gain, enc_w1, enc_w2).astype(jnp....  90 us
    all_to_all x1, blocking collectives, summed_on_arrival(): lax.all_to_all(in_blocks(value, dim, devices), axis, 0, 0, tiled=True)  34.5 us
    all_to_all x2, waiting for transfers between devices, copy_for_each(): return lax.all_to_all(copies, axis, split_axis=0, concat_axis=0, tiled=True)  24 us
    all_to_all x2, starting transfers between devices, copy_for_each(): return lax.all_to_all(copies, axis, split_axis=0, concat_axis=0, tiled=True)  10.4 us
    all_gather x1, waiting for transfers between devices, per_device(): lax.all_gather(out_weight, 'seq', axis=1, tiled=True)  10.2 us
    reshape x4, local copies, waits for them, and re-layouts, project_heads(): return result.reshape(span_count, NEIGH * RLEN, weight.shape[1] // HD, HD)  6.66 us
    dot_general x2, matrix products, project_heads(): jnp.dot(encoded, weight, preferred_element_type=jnp.float32)  5.82 us
    dot_general x1, matrix products, feed_partial(): return jnp.dot(inner, second_weight, preferred_element_type=jnp.float32)  5.5 us
  transfers between devices with their start and end apart: 6, of which 4 were waited for; matrix products, arithmetic and copies ran while one was open for 14% of the time, Pallas kernels for 0%

commit v1 on v0

v1 whole, which is shorter than its diff:
```python
import functools

import jax
import jax.numpy as jnp
from jax import lax
from jax.experimental import pallas as pl
from jax.experimental.pallas import tpu as pltpu
from jax.sharding import PartitionSpec as P

HD = 128
M = 64
BF = jnp.bfloat16
F32 = jnp.float32
MESH = pl.DeviceIdType.MESH

NX = 4
NZ = 8
ENC_A = 48
DEC_A = 96


def dot(a, b):
    return jnp.dot(a, b, preferred_element_type=F32)


def dot_t(a, b):
    return lax.dot_general(a, b, (((1,), (1,)), ((), ())), preferred_element_type=F32)


class Mover:
    def __init__(self, send, recv):
        self.send, self.recv = send, recv

    def copy(self, i, src, dst, device):
        return pltpu.make_async_remote_copy(
            src_ref=src,
            dst_ref=dst,
            send_sem=self.send.at[i],
            recv_sem=self.recv.at[i],
            device_id=device,
            device_id_type=MESH,
        )


def kernel(
    hid, nb, eg, w1, w2, wk, wv, dg, wq, wo, out,
    nbv, w1v, w2v, wkv, wvv, hbuf, wqb, wob,
    pbuf, ra, ryb, sb, rbx, sa, ray, ebuf,
    acc, qv, qn, qs, at, an, af,
    obuf, oa, oyb, osb, obx, osa, oay,
    lsem, hs, hr, es, er, rs, rr, bs, br, ws, wr, xs, xr,
):
    s = lax.axis_index("seq")
    t = lax.axis_index("tp")
    x, h = lax.div(t, 2), lax.rem(t, 2)
    yl, zc = lax.div(s, 16), lax.rem(s, 16)
    z, c = lax.div(zc, 2), lax.rem(zc, 2)
    nseq = lax.axis_size("seq")

    def at_x(k):
        return lax.rem(x + k, NX)

    def dev_x(k):
        return (s, at_x(k) * 2 + h)

    dev_h = (s, x * 2 + 1 - h)

    def at_z(k):
        return lax.rem(z + k + NZ, NZ)

    def dev_z(k):
        return (yl * 16 + at_z(k) * 2 + c, t)

    dev_c = (yl * 16 + z * 2 + 1 - c, t)
    dev_yl = ((1 - yl) * 16 + zc, t)
    dev_next = (lax.rem(s + 1, nseq), t)
    dev_prev = (lax.rem(s + nseq - 1, nseq), t)

    def local(i, src, dst):
        return pltpu.make_async_copy(src, dst, lsem.at[i])

    c_hid = local(0, hid, hbuf.at[x, h])
    c_wq = local(1, wq, wqb.at[yl, zc])
    c_w1 = local(2, w1, w1v)
    c_w2 = local(3, w2, w2v)
    c_wo = local(4, wo, wob.at[yl, zc])
    c_wk = local(5, wk, wkv)
    c_wv = local(6, wv, wvv)

    def c_nb(o):
        return local(7 + o, nb.at[at_x(o)], nbv.at[at_x(o)])

    c_hid.start()
    c_wq.start()
    c_nb(3).start()
    c_w1.start()
    c_w2.start()
    c_nb(2).start()
    c_nb(1).start()
    c_nb(0).start()
    c_wo.start()
    c_wk.start()
    c_wv.start()

    barrier = pltpu.get_barrier_semaphore()
    partners = [dev_x(1), dev_x(2), dev_x(3), dev_h, dev_z(1), dev_z(-1), dev_c, dev_yl, dev_next, dev_prev]
    for device in partners:
        pl.semaphore_signal(barrier, inc=1, device_id=device, device_id_type=MESH)
    pl.semaphore_wait(barrier, len(partners))

    started = []

    def go(cp):
        cp.start()
        started.append(cp)

    def ag_own(mv, buf, k):
        return mv.copy(k, buf.at[x, h], buf.at[x, h], dev_h if k == 0 else dev_x(k))

    def ag_own_in(mv, buf, k):
        ref = buf.at[x, 1 - h] if k == 0 else buf.at[at_x(NX - k), h]
        return mv.copy(k, ref, ref, dev_h)

    def ag_a(mv, buf, a, k):
        ref = buf.at[x, 1 - h, pl.ds(0, a)]
        return mv.copy(3 + k, ref, ref, dev_x(k))

    def ag_a_in(mv, buf, a, k):
        ref = buf.at[at_x(NX - k), 1 - h, pl.ds(0, a)]
        return mv.copy(3 + k, ref, ref, dev_h)

    def ag_b(mv, buf, a, k):
        rows = buf.shape[2]
        ref = buf.at[at_x(NX - k), h, pl.ds(a, rows - a)]
        return mv.copy(6 + k, ref, ref, dev_h)

    def ag_b_in(mv, buf, a, k):
        rows = buf.shape[2]
        ref = buf.at[at_x(NX - k), 1 - h, pl.ds(a, rows - a)]
        return mv.copy(6 + k, ref, ref, dev_h)

    hm, em = Mover(hs, hr), Mover(es, er)

    def ag_start(mv, buf):
        for k in (0, 1, 3, 2):
            go(ag_own(mv, buf, k))

    def ag_pass_a(mv, buf, a):
        ag_own_in(mv, buf, 0).wait_recv()
        for k in (1, 3, 2):
            go(ag_a(mv, buf, a, k))

    def ag_pass_b(mv, buf, a, k):
        ag_own_in(mv, buf, k).wait_recv()
        go(ag_b(mv, buf, a, k))

    def w_mover(i):
        return Mover(ws.at[i], wr.at[i])

    def blk(buf, cls, zz):
        return buf.at[cls, zz * 2 + c]

    def pair(buf, zz):
        return buf.at[:, zz * 2 + c]

    def same(mv, i, ref, device):
        return mv.copy(i, ref, ref, device)

    def w_start(i, buf):
        mv = w_mover(i)
        own = blk(buf, yl, z)
        go(same(mv, 0, own, dev_yl))
        go(same(mv, 1, own, dev_z(1)))
        go(same(mv, 6, own, dev_z(-1)))
        go(same(mv, 11, own, dev_c))

    def w_yl(i, buf):
        mv = w_mover(i)
        other = blk(buf, 1 - yl, z)
        same(mv, 0, other, dev_yl).wait_recv()
        go(same(mv, 2, other, dev_z(1)))
        go(same(mv, 7, other, dev_z(-1)))
        go(same(mv, 12, other, dev_c))

    def w_step(i, buf, k):
        mv = w_mover(i)
        for sign, base in ((-1, 1), (1, 6)):
            zz = at_z(sign * (k + 1))
            to = dev_z(-sign)
            cls = yl if sign < 0 else 1 - yl
            if k == 0:
                same(mv, base, blk(buf, yl, zz), to).wait_recv()
                same(mv, base + 1, blk(buf, 1 - yl, zz), to).wait_recv()
            elif k < 3:
                same(mv, base + 1 + k, pair(buf, zz), to).wait_recv()
            else:
                same(mv, base + 4, blk(buf, cls, zz), to).wait_recv()
            if k < 2:
                go(same(mv, base + 2 + k, pair(buf, zz), to))
            elif k == 2:
                go(same(mv, base + 4, blk(buf, cls, zz), to))
            ci = 13 + 2 * k + (0 if sign < 0 else 1)
            go(same(mv, ci, pair(buf, zz) if k < 3 else blk(buf, cls, zz), dev_c))

    def w_finish(i, buf):
        mv = w_mover(i)

        def theirs(cls, zz):
            return buf.at[cls, zz * 2 + 1 - c]

        def theirs2(zz):
            return buf.at[:, zz * 2 + 1 - c]

        same(mv, 11, theirs(yl, z), dev_c).wait_recv()
        same(mv, 12, theirs(1 - yl, z), dev_c).wait_recv()
        for k in range(4):
            for sign in (-1, 1):
                zz = at_z(sign * (k + 1))
                cls = yl if sign < 0 else 1 - yl
                ci = 13 + 2 * k + (0 if sign < 0 else 1)
                same(mv, ci, theirs2(zz) if k < 3 else theirs(cls, zz), dev_c).wait_recv()

    def rs_a(mv, part, land, a, o):
        return mv.copy(o, part.at[at_x(o), :, pl.ds(0, a)], land.at[o - 1], dev_x(o))

    def rs_b(mv, part, land, a, o):
        rows = part.shape[2]
        cc = at_x(o)
        return mv.copy(4 + o, part.at[cc, 1 - h, pl.ds(a, rows - a)], land.at[cc], dev_h)

    def rs_sends(mv, part, land_a, land_b, a, o):
        rs_b(mv, part, land_b, a, o).start()

        @pl.when(o > 0)
        def _():
            rs_a(mv, part, land_a, a, o).start()

    def rs_middle(mv, part, land_a, land_b, sum_b, land_bx, sum_a, land_ay, a):
        rows = part.shape[2]
        for o in (3, 2, 1):
            cc = at_x(o)
            rs_b(mv, part, land_b, a, o).wait_recv()
            sum_b[o - 1] = (part[cc, h, a:rows].astype(F32) + land_b[cc].astype(F32)).astype(BF)
            go(mv.copy(8 + o, sum_b.at[o - 1], land_bx.at[o - 1], dev_x(o)))
        for o in (3, 1, 2):
            rs_a(mv, part, land_a, a, o).wait_recv()
        total = part[x, 1 - h, 0:a].astype(F32)
        for o in (1, 2, 3):
            total += land_a[o - 1, 1 - h].astype(F32)
        sum_a[...] = total.astype(BF)
        go(mv.copy(8, sum_a, land_ay, dev_h))
        rs_b(mv, part, land_b, a, 0).wait_recv()

    def rs_last(mv, part, land_a, land_b, sum_b, land_bx, sum_a, land_ay, a):
        rows = part.shape[2]
        tb = part[x, h, a:rows].astype(F32) + land_b[x].astype(F32)
        for o in (1, 3, 2):
            mv.copy(8 + o, sum_b.at[o - 1], land_bx.at[o - 1], dev_x(o)).wait_recv()
            tb += land_bx[o - 1].astype(F32)
        ta = part[x, h, 0:a].astype(F32)
        for o in (1, 2, 3):
            ta += land_a[o - 1, h].astype(F32)
        mv.copy(8, sum_a, land_ay, dev_h).wait_recv()
        ta += land_ay[...].astype(F32)
        return ta, tb

    def rs_sent(mv, part, land_a, land_b, a):
        for o in range(4):
            rs_b(mv, part, land_b, a, o).wait_send()
            if o:
                rs_a(mv, part, land_a, a, o).wait_send()

    c_hid.wait()
    ag_start(hm, hbuf)
    c_wq.wait()
    w_start(0, wqb)
    c_w1.wait()
    c_w2.wait()

    rm, bm = Mover(rs, rr), Mover(bs, br)

    def enc_chunk(i, carry):
        o = 3 - i
        cc = at_x(o)
        c_nb(o).wait()
        v = nbv[cc].astype(F32)
        scale = lax.rsqrt(jnp.mean(v * v, axis=-1, keepdims=True) + 1e-06)
        norm = (v * scale * eg[...]).astype(BF)
        inner = jnp.maximum(dot_t(norm, w1v[...]), 0.0).astype(BF)
        pbuf[cc] = dot(inner, w2v[...]).astype(BF).reshape(2, 128, 896)
        rs_sends(rm, pbuf, ra, ryb, ENC_A, o)
        return carry

    lax.fori_loop(0, NX, enc_chunk, 0)

    w_yl(0, wqb)
    c_wo.wait()
    ag_pass_a(hm, hbuf, DEC_A)
    w_step(0, wqb, 0)
    w_start(1, wob)
    for k in (1, 3, 2):
        ag_pass_b(hm, hbuf, DEC_A, k)
    enc_rs = (rm, pbuf, ra, ryb, sb, rbx, sa, ray, ENC_A)
    rs_middle(*enc_rs)
    w_step(0, wqb, 1)
    w_yl(1, wob)
    ta, tb = rs_last(*enc_rs)
    ebuf[x, h, 0:ENC_A] = (nbv[x, pl.ds(pl.multiple_of(h * 128, 128), ENC_A)].astype(F32) + ta).astype(BF)
    ebuf[x, h, ENC_A:128] = (
        nbv[x, pl.ds(pl.multiple_of(h * 128 + ENC_A, 16), 128 - ENC_A)].astype(F32) + tb
    ).astype(BF)
    ag_start(em, ebuf)
    w_step(0, wqb, 2)
    w_step(1, wob, 0)
    w_step(0, wqb, 3)
    ag_pass_a(em, ebuf, ENC_A)
    for k in (1, 2, 3):
        ag_a_in(hm, hbuf, DEC_A, k).wait_recv()
        ag_b_in(hm, hbuf, DEC_A, k).wait_recv()
    w_finish(0, wqb)

    total = jnp.zeros((256, 1), F32)
    for i in range(8):
        v = hbuf[i // 2, i % 2].astype(F32)
        total += jnp.sum(v * v, axis=-1, keepdims=True)
    scale = lax.rsqrt(total * (1.0 / 4096.0) + 1e-06)
    acc[...] = jnp.zeros_like(acc)

    def query_block(i, carry):
        v = hbuf[lax.div(i, 2), lax.rem(i, 2)].astype(F32)
        norm = (v * scale * dg[i]).astype(BF)
        w = wqb[lax.div(i, 4), pl.ds(lax.rem(i, 4) * 4, 4)].reshape(512, 512)
        acc[...] += dot(norm, w)
        return carry

    lax.fori_loop(0, 8, query_block, 0)
    qv[...] = acc[...].astype(BF)
    xm = Mover(xs, xr)
    q_halo = xm.copy(0, qv.at[pl.ds(0, M)], qn, dev_prev)
    go(q_halo)
    w_step(1, wob, 1)
    for k in (1, 3, 2):
        ag_pass_b(em, ebuf, ENC_A, k)
    q_halo.wait_recv()
    joined = jnp.concatenate([qv[...].astype(F32), qn[...].astype(F32)], axis=0)
    qs[...] = pltpu.roll(joined, 1, 0)[M : M + 256].astype(BF)
    c_wk.wait()
    c_wv.wait()

    a_halo = xm.copy(1, at.at[pl.ds(3 * M, M)], an, dev_next)

    def span(o, carry):
        cc = at_x(NX - o)

        @pl.when(o > 0)
        def _():
            ag_a_in(em, ebuf, ENC_A, o).wait_recv()
            ag_b_in(em, ebuf, ENC_A, o).wait_recv()

        e = ebuf[cc].reshape(256, 896)
        keys = dot(e, wkv[...]).astype(BF)
        values = dot(e, wvv[...]).astype(BF)
        rows = pl.ds(pl.multiple_of(cc * M, M), M)
        q = qs[rows]
        for j in range(4):
            cols = slice(j * HD, (j + 1) * HD)
            scores = dot_t(q[:, cols], keys[:, cols]) * HD ** (-0.5)
            ex = jnp.exp(scores - jnp.max(scores, axis=-1, keepdims=True))
            probs = (ex / jnp.sum(ex, axis=-1, keepdims=True)).astype(BF)
            at[rows, cols] = dot(probs, values[:, cols]).astype(BF)

        @pl.when(cc == 3)
        def _():
            a_halo.start()

        return carry

    lax.fori_loop(0, NX, span, 0)
    w_step(1, wob, 2)
    w_step(1, wob, 3)
    a_halo.wait_recv()
    joined = jnp.concatenate([an[...].astype(F32), at[0:200].astype(F32)], axis=0)
    mine = pltpu.roll(joined, 263, 0)[0:256]
    position = s * 256 + lax.broadcasted_iota(jnp.int32, (256, 512), 0)
    af[...] = jnp.where(position >= M - 1, mine, 0.0).astype(BF)
    w_finish(1, wob)

    def out_block(i, carry):
        o = 3 - i
        cc = at_x(o)
        for hh in range(2):
            tt = cc * 2 + hh
            first = lax.rem(tt, 4) * 4
            w = jnp.concatenate([wob[lax.div(tt, 4), first + n] for n in range(4)], axis=1)
            obuf[cc, hh] = dot(af[...], w).astype(BF)
        rs_sends(bm, obuf, oa, oyb, DEC_A, o)
        return carry

    lax.fori_loop(0, NX, out_block, 0)
    dec_rs = (bm, obuf, oa, oyb, osb, obx, osa, oay, DEC_A)
    rs_middle(*dec_rs)
    ta, tb = rs_last(*dec_rs)
    out[0:DEC_A] = (hbuf[x, h, 0:DEC_A].astype(F32) + ta).astype(BF)
    out[DEC_A:256] = (hbuf[x, h, DEC_A:256].astype(F32) + tb).astype(BF)

    for cp in started:
        cp.wait_send()
    a_halo.wait_send()
    rs_sent(rm, pbuf, ra, ryb, ENC_A)
    rs_sent(bm, obuf, oa, oyb, DEC_A)


def per_device(hidden, neighbours, enc_gain, enc_w1, enc_w2, key_weight, value_weight, dec_gain, query_weight, out_weight):
    dma = pltpu.SemaphoreType.DMA
    ea, eb, da, db = ENC_A, 128 - ENC_A, DEC_A, 256 - DEC_A
    V = pltpu.VMEM
    any_ = pl.BlockSpec(memory_space=pl.ANY)
    vm = pl.BlockSpec(memory_space=pltpu.VMEM)
    return pl.pallas_call(
        kernel,
        out_shape=jax.ShapeDtypeStruct((256, 512), BF),
        in_specs=[any_, any_, vm, any_, any_, any_, any_, vm, any_, any_],
        out_specs=vm,
        scratch_shapes=[
            V((4, 256, 896), BF), V((448, 896), BF), V((448, 896), BF), V((896, 512), BF), V((896, 512), BF),
            V((4, 2, 256, 512), BF), V((2, 16, 128, 512), BF), V((2, 16, 512, 128), BF),
            V((4, 2, 128, 896), BF), V((3, 2, ea, 896), BF), V((4, eb, 896), BF), V((3, eb, 896), BF),
            V((3, eb, 896), BF), V((ea, 896), BF), V((ea, 896), BF), V((4, 2, 128, 896), BF),
            V((256, 512), F32), V((256, 512), BF), V((64, 512), BF), V((256, 512), BF), V((256, 512), BF),
            V((64, 512), BF), V((256, 512), BF),
            V((4, 2, 256, 512), BF), V((3, 2, da, 512), BF), V((4, db, 512), BF), V((3, db, 512), BF),
            V((3, db, 512), BF), V((da, 512), BF), V((da, 512), BF),
            dma((11,)), dma((10,)), dma((10,)), dma((10,)), dma((10,)), dma((12,)), dma((12,)), dma((12,)), dma((12,)),
            dma((2, 21)), dma((2, 21)), dma((2,)), dma((2,)),
        ],
        compiler_params=pltpu.CompilerParams(collective_id=0, has_side_effects=True, vmem_limit_bytes=60 * 1024 * 1024),
        name="layer",
    )(
        hidden, neighbours, enc_gain.reshape(1, -1), enc_w1.T, enc_w2, key_weight, value_weight,
        dec_gain.reshape(8, 1, 512), query_weight, out_weight,
    )


def solution(mesh):
    placed = (
        P("seq", "tp"), P("seq", None, None), P(), P(None, "tp"), P("tp", None), P(None, "tp"), P(None, "tp"), P(),
        P("seq", "tp"), P("tp", "seq"),
    )
    return jax.shard_map(per_device, mesh=mesh, in_specs=placed, out_specs=P("seq", "tp"), check_vma=False)
```

time: 239 us -> 108 us (0.45)
  waiting for transfers between devices: 127 us -> 0 us
  Pallas kernels: 0 us -> 103 us
  blocking collectives: 34.5 us -> 0 us
  matrix products: 23.6 us -> 0 us
  between operations: 15 us -> 0.01 us
  local copies, waits for them, and re-layouts: 15.7 us -> 2.94 us
  starting transfers between devices: 12.6 us -> 0 us
  other arithmetic: 10.1 us -> 0 us
    pallas_call x0 -> x1, Pallas kernels: none -> 103 us  [per_device(): pl.pallas_call(kernel, out_shape=jax.ShapeDtypeStruct((256, 512), BF), in...]
    reduce_scatter x1 -> x0, waiting for transfers between devices: 90 us -> none  [encode(): lax.psum_scatter(feed_partial(flat, enc_gain, enc_w1, enc_w2).astype(jnp....]
    all_to_all x1 -> x0, blocking collectives: 34.5 us -> none  [summed_on_arrival(): lax.all_to_all(in_blocks(value, dim, devices), axis, 0, 0, tiled=True)]
    all_to_all x2 -> x0, waiting for transfers between devices: 24 us -> none  [copy_for_each(): return lax.all_to_all(copies, axis, split_axis=0, concat_axis=0, tiled=True)]
    dot_general x6 -> x0, matrix products: 20.7 us -> none  [the longest x2 5.82 us: project_heads(): jnp.dot(encoded, weight, preferred_element_type=jnp.float32)]
    all_to_all x2 -> x0, starting transfers between devices: 10.4 us -> none  [copy_for_each(): return lax.all_to_all(copies, axis, split_axis=0, concat_axis=0, tiled=True)]
    all_gather x2 -> x0, waiting for transfers between devices: 10.2 us -> none  [the longest x1 10.2 us: per_device(): lax.all_gather(out_weight, 'seq', axis=1, tiled=True)]
    reshape x6 -> x1, local copies, waits for them, and re-layouts: 7.68 us -> 1.27 us  [per_device(): enc_gain.reshape(1, -1)]
  transfers between devices with their start and end apart: 6 -> 0, of which waited for: 4 -> 0; matrix products, arithmetic and copies ran while one was open for 14% -> 0% of each run, Pallas kernels for 0% -> 0%
where the time goes in v1:
time: 108 us; the launch traced here: 106 us
  Pallas kernels  103 us (95%)
  local copies, waits for them, and re-layouts  2.94 us (3%)
    pallas_call x1, Pallas kernels, per_device(): pl.pallas_call(kernel, out_shape=jax.ShapeDtypeStruct((256, 512), BF), in...  103 us

profile of v1, /device:TPU:8, one launch (start us, length us, event | category | flops | bytes accessed | tf_op | source)
XLA Modules:
  0.0 105.6 jit_solution(3364325854556888287)
XLA Ops:
  0.0 1.3 %reshape.6.eg = f32[1,896]{1,0:T(1,128)} reshape(f32[896]{0:T(1024)} %param.12) | data formatting | bytes 7168 | tf_op jit(solution)/shard_map/reshape | solution.py:439
  1.3 102.7 %layer.1 = bf16[256,512]{1,0:T(8,128)(2,1)} custom-call(bf16[256,512]{1,0:T(8,128)(2,1)} %hid.1, bf16[4,256,896]{2,1,0:T(8,128)(2,1)} %nb.1, f32[1,896]{1,0:T(1,128)} %reshape.6.eg, bf16[448,896]{1,0:T(8,128)(2,1)} %bitcast.2, bf16[448,896]{1,0:T(8,128)(2,1)} %w2.1, bf16[896,512]{1,0:T(8,128)(2,1)} %wk.1, bf16[896,512]{1,0:T(8,128)(2,1)} %wv.1, ...), custom_call_target="tpu_custom_call" | custom-call | tf_op jit(solution)/shard_map/layer/pallas_call | solution.py:419
  104.0 1.7 %copy.12 = bf16[256,512]{1,0:T(8,128)(2,1)} copy(bf16[256,512]{1,0:T(8,128)(2,1)} %layer.1) | data formatting | bytes 524288

commit v2 on v1

v2 whole, which is shorter than its diff:
```python
import functools

import jax
import jax.numpy as jnp
from jax import lax
from jax.experimental import pallas as pl
from jax.experimental.pallas import tpu as pltpu
from jax.sharding import PartitionSpec as P

HD = 128
M = 64
BF = jnp.bfloat16
F32 = jnp.float32
MESH = pl.DeviceIdType.MESH

NX = 4
NZ = 8
ENC_A = 64
DEC_A = 128


def dot(a, b):
    return jnp.dot(a, b, preferred_element_type=F32)


def dot_t(a, b):
    return lax.dot_general(a, b, (((1,), (1,)), ((), ())), preferred_element_type=F32)


class Mover:
    def __init__(self, send, recv):
        self.send, self.recv = send, recv

    def copy(self, i, src, dst, device):
        return pltpu.make_async_remote_copy(
            src_ref=src,
            dst_ref=dst,
            send_sem=self.send.at[i],
            recv_sem=self.recv.at[i],
            device_id=device,
            device_id_type=MESH,
        )


def kernel(
    hid, nb, eg, w1, w2, wk, wv, dg, wq, wo, out,
    nbv, w1v, w2v, wkv, wvv, hbuf, wqb, wob,
    pbuf, ra, ryb, sb, rbx, sa, ray, ebuf,
    acc, qv, qn, qs, at, an, af,
    obuf, oin, own,
    lsem, hs, hr, es, er, rs, rr, bs, br, ws, wr, xs, xr,
):
    s = lax.axis_index("seq")
    t = lax.axis_index("tp")
    x, h = lax.div(t, 2), lax.rem(t, 2)
    yl, zc = lax.div(s, 16), lax.rem(s, 16)
    z, c = lax.div(zc, 2), lax.rem(zc, 2)
    nseq = lax.axis_size("seq")

    def at_x(k):
        return lax.rem(x + k, NX)

    def dev_x(k):
        return (s, at_x(k) * 2 + h)

    dev_h = (s, x * 2 + 1 - h)

    def active(zz):
        return lax.rem(lax.div(zz, 2), 2) == h

    def slot(zz):
        return lax.div(zz, 4) * 2 + lax.rem(zz, 2)

    def at_z(k):
        return lax.rem(z + k + NZ, NZ)

    def dev_z(k):
        return (yl * 16 + at_z(k) * 2 + c, t)

    dev_c = (yl * 16 + z * 2 + 1 - c, t)
    dev_yl = ((1 - yl) * 16 + zc, t)
    dev_next = (lax.rem(s + 1, nseq), t)
    dev_prev = (lax.rem(s + nseq - 1, nseq), t)
    dev_next_h = (lax.rem(s + 1, nseq), x * 2 + 1 - h)
    dev_prev_h = (lax.rem(s + nseq - 1, nseq), x * 2 + 1 - h)

    def local(i, src, dst):
        return pltpu.make_async_copy(src, dst, lsem.at[i])

    c_hid = local(0, hid, hbuf.at[x, h])
    c_wq = local(1, wq, wqb.at[yl, zc])
    c_w1 = local(2, w1, w1v)
    c_w2 = local(3, w2, w2v)
    c_wo = local(4, wo, wob.at[yl, slot(z), c, h])
    c_wk = local(5, wk, wkv)
    c_wv = local(6, wv, wvv)

    def c_nb(o):
        return local(7 + o, nb.at[at_x(o)], nbv.at[at_x(o)])

    c_hid.start()
    c_wq.start()
    c_nb(3).start()
    c_w1.start()
    c_w2.start()
    c_nb(2).start()
    c_nb(1).start()
    c_nb(0).start()

    @pl.when(active(z))
    def _():
        c_wo.start()

    c_wk.start()
    c_wv.start()

    barrier = pltpu.get_barrier_semaphore()
    partners = [dev_x(1), dev_x(2), dev_x(3), dev_h, dev_z(1), dev_z(-1), dev_c, dev_yl, dev_next, dev_prev, dev_next_h, dev_prev_h]
    for device in partners:
        pl.semaphore_signal(barrier, inc=1, device_id=device, device_id_type=MESH)
    pl.semaphore_wait(barrier, len(partners))

    started = []

    def go(cp, cond=None):
        if cond is None:
            cp.start()
        else:
            pl.when(cond)(cp.start)
        started.append((cp, cond))

    class Gather:
        def __init__(self, mv, buf, first):
            self.mv, self.buf, self.a, self.b = mv, buf, first, buf.shape[2] - first

        def at(self, i, cc, hh, top, device):
            ref = self.buf.at[cc, hh, pl.ds(0, self.a) if top else pl.ds(self.a, self.b)]
            return self.mv.copy(i, ref, ref, device)

        def first_a(self):
            go(self.at(0, x, h, True, dev_h))

        def first_b(self):
            for k in (2, 1, 3):
                go(self.at(k, x, h, False, dev_x(k)))

        def own_a(self):
            for k in (2, 1, 3):
                go(self.at(3 + k, x, h, True, dev_x(k)))

        def own_b(self):
            go(self.at(7, x, h, False, dev_h))

        def pass_a(self):
            self.at(0, x, 1 - h, True, dev_h).wait_recv()
            for k in (2, 1, 3):
                go(self.at(7 + k, x, 1 - h, True, dev_x(k)))

        def pass_b(self, k):
            self.at(k, at_x(NX - k), h, False, dev_h).wait_recv()
            go(self.at(10 + k, at_x(NX - k), h, False, dev_h))

        def near(self):
            self.at(7, x, 1 - h, False, dev_h).wait_recv()

        def rest(self, k):
            cc = at_x(NX - k)
            self.at(3 + k, cc, h, True, dev_h).wait_recv()
            self.at(7 + k, cc, 1 - h, True, dev_h).wait_recv()
            self.at(10 + k, cc, 1 - h, False, dev_h).wait_recv()

    def when(cond, f):
        if cond is None:
            f()
        else:
            pl.when(cond)(f)

    class Ring:
        def __init__(self, i, unit, here):
            self.mv, self.unit, self.here = Mover(ws.at[i], wr.at[i]), unit, here

        def same(self, i, ref, device):
            return self.mv.copy(i, ref, ref, device)

        def start(self):
            own, on = self.unit(yl, z, c), self.here(z)
            go(self.same(0, own, dev_yl), on)
            go(self.same(1, own, dev_z(1)), on)
            go(self.same(8, own, dev_z(-1)), on)
            go(self.same(15, own, dev_c), on)

        def across(self):
            other, on = self.unit(1 - yl, z, c), self.here(z)
            when(on, self.same(0, other, dev_yl).wait_recv)
            go(self.same(2, other, dev_z(1)), on)
            go(self.same(9, other, dev_z(-1)), on)
            go(self.same(16, other, dev_c), on)

        def step(self, k, other):
            for d, sign in enumerate((-1, 1)):
                if k == 3 and other != d:
                    continue
                zz = at_z(sign * (k + 1))
                to, on = dev_z(-sign), self.here(zz)
                ref = self.unit(1 - yl if other else yl, zz, c)
                i = 1 + 7 * d + (6 if k == 3 else 2 * k + other)
                when(on, self.same(i, ref, to).wait_recv)
                if k < 2 or (k == 2 and other == d):
                    go(self.same(1 + 7 * d + (6 if k == 2 else 2 * k + 2 + other), ref, to), on)
                go(self.same(17 + 4 * k + (d if k == 3 else 2 * d + other), ref, dev_c), on)

        def finish(self):
            def wait(i, cls, zz):
                when(self.here(zz), self.same(i, self.unit(cls, zz, 1 - c), dev_c).wait_recv)

            wait(15, yl, z)
            wait(16, 1 - yl, z)
            for k in range(4):
                for d, sign in enumerate((-1, 1)):
                    for other in range(2):
                        if k == 3 and other != d:
                            continue
                        i = 17 + 4 * k + (d if k == 3 else 2 * d + other)
                        wait(i, 1 - yl if other else yl, at_z(sign * (k + 1)))

    def rs_a(mv, part, land, a, o):
        return mv.copy(o, part.at[at_x(o), :, pl.ds(0, a)], land.at[o - 1], dev_x(o))

    def rs_b(mv, part, land, a, o):
        rows = part.shape[2]
        cc = at_x(o)
        return mv.copy(4 + o, part.at[cc, 1 - h, pl.ds(a, rows - a)], land.at[cc], dev_h)

    def rs_sends(mv, part, land_a, land_b, a, o):
        rs_b(mv, part, land_b, a, o).start()

        @pl.when(o > 0)
        def _():
            rs_a(mv, part, land_a, a, o).start()

    def rs_middle(mv, part, land_a, land_b, sum_b, land_bx, sum_a, land_ay, a):
        rows = part.shape[2]
        for o in (3, 2, 1):
            cc = at_x(o)
            rs_b(mv, part, land_b, a, o).wait_recv()
            sum_b[o - 1] = (part[cc, h, a:rows].astype(F32) + land_b[cc].astype(F32)).astype(BF)
            go(mv.copy(8 + o, sum_b.at[o - 1], land_bx.at[o - 1], dev_x(o)))
        for o in (3, 1, 2):
            rs_a(mv, part, land_a, a, o).wait_recv()
        total = part[x, 1 - h, 0:a].astype(F32)
        for o in (1, 2, 3):
            total += land_a[o - 1, 1 - h].astype(F32)
        sum_a[...] = total.astype(BF)
        go(mv.copy(8, sum_a, land_ay, dev_h))
        rs_b(mv, part, land_b, a, 0).wait_recv()

    def rs_last(mv, part, land_a, land_b, sum_b, land_bx, sum_a, land_ay, a):
        rows = part.shape[2]
        tb = part[x, h, a:rows].astype(F32) + land_b[x].astype(F32)
        for o in (1, 3, 2):
            mv.copy(8 + o, sum_b.at[o - 1], land_bx.at[o - 1], dev_x(o)).wait_recv()
            tb += land_bx[o - 1].astype(F32)
        ta = part[x, h, 0:a].astype(F32)
        for o in (1, 2, 3):
            ta += land_a[o - 1, h].astype(F32)
        mv.copy(8, sum_a, land_ay, dev_h).wait_recv()
        ta += land_ay[...].astype(F32)
        return ta, tb

    def rs_sent(mv, part, land_a, land_b, a):
        for o in range(4):
            rs_b(mv, part, land_b, a, o).wait_send()
            if o:
                rs_a(mv, part, land_a, a, o).wait_send()

    rm, bm, xm = Mover(rs, rr), Mover(bs, br), Mover(xs, xr)
    gd, ge = Gather(Mover(hs, hr), hbuf, DEC_A), Gather(Mover(es, er), ebuf, ENC_A)
    rq = Ring(0, lambda cls, zz, core: wqb.at[cls, zz * 2 + core], lambda zz: None)
    ro = Ring(1, lambda cls, zz, core: wob.at[cls, slot(zz), core], active)

    c_wq.wait()
    rq.start()
    theirs = wob.at[yl, slot(z), c, h]
    go(ro.mv.copy(31, wo, theirs, dev_h), jnp.logical_not(active(z)))
    c_hid.wait()
    gd.first_a()
    gd.first_b()
    c_w1.wait()
    c_w2.wait()

    def enc_chunk(i, carry):
        o = 3 - i
        cc = at_x(o)
        c_nb(o).wait()
        v = nbv[cc].astype(F32)
        scale = lax.rsqrt(jnp.mean(v * v, axis=-1, keepdims=True) + 1e-06)
        norm = (v * scale * eg[...].reshape(1, 896)).astype(BF)
        inner = jnp.maximum(dot_t(norm, w1v[...]), 0.0).astype(BF)
        pbuf[cc] = dot(inner, w2v[...]).astype(BF).reshape(2, 128, 896)
        rs_sends(rm, pbuf, ra, ryb, ENC_A, o)
        return carry

    lax.fori_loop(0, NX, enc_chunk, 0)

    rq.across()

    @pl.when(active(z))
    def _():
        c_wo.wait()
        handed = wob.at[yl, slot(z), c, 1 - h]
        ro.mv.copy(31, handed, handed, dev_h).wait_recv()

    ro.start()
    gd.own_a()
    gd.own_b()
    rq.step(0, 0)
    rq.step(0, 1)
    rq.step(1, 0)
    rq.step(1, 1)
    enc_rs = (rm, pbuf, ra, ryb, sb, rbx, sa, ray, ENC_A)
    rs_middle(*enc_rs)
    gd.pass_a()
    for k in (1, 3, 2):
        gd.pass_b(k)
    ro.step(0, 0)
    rq.step(2, 0)
    rq.step(2, 1)
    ro.across()
    ta, tb = rs_last(*enc_rs)
    ebuf[x, h, 0:ENC_A] = (nbv[x, pl.ds(pl.multiple_of(h * 128, 128), ENC_A)].astype(F32) + ta).astype(BF)
    ge.first_a()
    ebuf[x, h, ENC_A:128] = (
        nbv[x, pl.ds(pl.multiple_of(h * 128 + ENC_A, 16), 128 - ENC_A)].astype(F32) + tb
    ).astype(BF)
    ge.first_b()
    ge.own_a()
    ge.own_b()
    rq.step(3, 0)
    rq.step(3, 1)
    ro.step(1, 0)
    ge.pass_a()
    ro.step(0, 1)
    gd.near()
    for k in (1, 3, 2):
        gd.rest(k)
    rq.finish()

    total = jnp.zeros((256, 1), F32)
    for i in range(8):
        v = hbuf[i // 2, i % 2].astype(F32)
        total += jnp.sum(v * v, axis=-1, keepdims=True)
    scale = lax.rsqrt(total * (1.0 / 4096.0) + 1e-06)
    acc[...] = jnp.zeros_like(acc)

    def query_block(i, carry):
        v = hbuf[lax.div(i, 2), lax.rem(i, 2)].astype(F32)
        norm = (v * scale * dg[i]).astype(BF)
        w = wqb[lax.div(i, 4), pl.ds(lax.rem(i, 4) * 4, 4)].reshape(512, 512)
        acc[...] += dot(norm, w)
        return carry

    lax.fori_loop(0, 8, query_block, 0)
    qv[...] = acc[...].astype(BF)
    q_halo = xm.copy(0, qv.at[pl.ds(0, M)], qn, dev_prev)
    go(q_halo)
    for k in (1, 3, 2):
        ge.pass_b(k)
    ro.step(2, 0)
    ro.step(1, 1)
    c_wk.wait()
    c_wv.wait()
    q_halo.wait_recv()
    joined = jnp.concatenate([qv[...].astype(F32), qn[...].astype(F32)], axis=0)
    qs[...] = pltpu.roll(joined, 1, 0)[M : M + 256].astype(BF)

    def at_copy(cc):
        rows = pl.ds(pl.multiple_of(cc * M, M), M)
        return xm.copy(4 + cc, at.at[h, rows], at.at[h, rows], dev_h)

    def at_copy_in(cc):
        rows = pl.ds(pl.multiple_of(cc * M, M), M)
        return xm.copy(4 + cc, at.at[1 - h, rows], at.at[1 - h, rows], dev_h)

    a_halo = xm.copy(1, at.at[h, pl.ds(3 * M, M)], an.at[h], dev_next)
    a_halo_h = xm.copy(8, at.at[h, pl.ds(3 * M, M)], an.at[h], dev_next_h)

    def span(o, carry):
        cc = at_x(NX - o)

        @pl.when(o > 0)
        def _():
            ge.rest(o)

        @pl.when(o == 0)
        def _():
            ge.near()

        e = ebuf[cc].reshape(256, 896)
        keys = dot(e, wkv[...]).astype(BF)
        values = dot(e, wvv[...]).astype(BF)
        rows = pl.ds(pl.multiple_of(cc * M, M), M)
        q = qs[rows]
        for j in range(4):
            cols = slice(j * HD, (j + 1) * HD)
            scores = dot_t(q[:, cols], keys[:, cols]) * HD ** (-0.5)
            ex = jnp.exp(scores - jnp.max(scores, axis=-1, keepdims=True))
            probs = (ex / jnp.sum(ex, axis=-1, keepdims=True)).astype(BF)
            at[h, rows, cols] = dot(probs, values[:, cols]).astype(BF)

        @pl.when(cc == 3)
        def _():
            a_halo.start()
            a_halo_h.start()

        at_copy(cc).start()
        return carry

    lax.fori_loop(0, NX, span, 0)
    ro.step(3, 0)
    ro.step(2, 1)
    ro.step(3, 1)
    ro.finish()
    a_halo.wait_recv()
    xm.copy(8, an.at[1 - h], an.at[1 - h], dev_h).wait_recv()
    for cc in range(4):
        at_copy_in(cc).wait_recv()
    position = s * 256 + lax.broadcasted_iota(jnp.int32, (256, 512), 0)
    for hh in range(2):
        joined = jnp.concatenate([an[hh].astype(F32), at[hh, 0:200].astype(F32)], axis=0)
        mine = pltpu.roll(joined, 263, 0)[0:256]
        af[hh] = jnp.where(position >= M - 1, mine, 0.0).astype(BF)

    def o_copy(o):
        return bm.copy(o - 1, obuf.at[o - 1], oin.at[o - 1], dev_x(o))

    def out_block(i, carry):
        o = jnp.where(i == 0, 2, jnp.where(i == 1, 1, jnp.where(i == 2, 3, 0)))
        cc = at_x(o)
        part = jnp.zeros((256, 512), F32)
        for hh in range(2):
            first = lax.rem(cc, 2) * 2
            w = [wob[lax.div(cc, 2), first + n // 2, n % 2, hh] for n in range(4)]
            part += dot(af[hh], jnp.concatenate(w, axis=1))

        @pl.when(o > 0)
        def _():
            obuf[o - 1] = part.astype(BF)
            o_copy(o).start()

        @pl.when(o == 0)
        def _():
            own[...] = hbuf[x, h].astype(F32) + part

        return carry

    lax.fori_loop(0, NX, out_block, 0)
    for o in (1, 3, 2):
        o_copy(o).wait_recv()
    out[...] = (own[...] + oin[0].astype(F32) + oin[1].astype(F32) + oin[2].astype(F32)).astype(BF)

    for cp, cond in started:
        if cond is None:
            cp.wait_send()
        else:
            pl.when(cond)(cp.wait_send)
    a_halo.wait_send()
    a_halo_h.wait_send()
    for k in range(4):
        at_copy(k).wait_send()
        if k:
            o_copy(k).wait_send()
    rs_sent(rm, pbuf, ra, ryb, ENC_A)


def per_device(hidden, neighbours, enc_gain, enc_w1, enc_w2, key_weight, value_weight, dec_gain, query_weight, out_weight):
    dma = pltpu.SemaphoreType.DMA
    ea, eb = ENC_A, 128 - ENC_A
    V = pltpu.VMEM
    any_ = pl.BlockSpec(memory_space=pl.ANY)
    vm = pl.BlockSpec(memory_space=pltpu.VMEM)
    return pl.pallas_call(
        kernel,
        out_shape=jax.ShapeDtypeStruct((256, 512), BF),
        in_specs=[any_, any_, vm, any_, any_, any_, any_, vm, any_, any_],
        out_specs=vm,
        scratch_shapes=[
            V((4, 256, 896), BF), V((448, 896), BF), V((448, 896), BF), V((896, 512), BF), V((896, 512), BF),
            V((4, 2, 256, 512), BF), V((2, 16, 128, 512), BF), V((2, 4, 2, 2, 512, 128), BF),
            V((4, 2, 128, 896), BF), V((3, 2, ea, 896), BF), V((4, eb, 896), BF), V((3, eb, 896), BF),
            V((3, eb, 896), BF), V((ea, 896), BF), V((ea, 896), BF), V((4, 2, 128, 896), BF),
            V((256, 512), F32), V((256, 512), BF), V((64, 512), BF), V((256, 512), BF), V((2, 256, 512), BF),
            V((2, 64, 512), BF), V((2, 256, 512), BF),
            V((3, 256, 512), BF), V((3, 256, 512), BF), V((256, 512), F32),
            dma((11,)), dma((14,)), dma((14,)), dma((14,)), dma((14,)), dma((12,)), dma((12,)), dma((3,)), dma((3,)),
            dma((2, 32)), dma((2, 32)), dma((9,)), dma((9,)),
        ],
        compiler_params=pltpu.CompilerParams(collective_id=0, has_side_effects=True, vmem_limit_bytes=60 * 1024 * 1024),
        name="layer",
    )(
        hidden, neighbours, enc_gain, enc_w1.T, enc_w2, key_weight, value_weight,
        dec_gain.reshape(8, 1, 512), query_weight, out_weight,
    )


def solution(mesh):
    placed = (
        P("seq", "tp"), P("seq", None, None), P(), P(None, "tp"), P("tp", None), P(None, "tp"), P(None, "tp"), P(),
        P("seq", "tp"), P("tp", "seq"),
    )
    return jax.shard_map(per_device, mesh=mesh, in_specs=placed, out_specs=P("seq", "tp"), check_vma=False)
```

time: 108 us -> 92.7 us (0.86)
  Pallas kernels: 103 us -> 89.3 us
  local copies, waits for them, and re-layouts: 2.94 us -> 1.67 us
    pallas_call x1, Pallas kernels: 103 us -> 89.3 us  [per_device(): pl.pallas_call(kernel, out_shape=jax.ShapeDtypeStruct((256, 512), BF), in...]
    reshape x1 -> x0, local copies, waits for them, and re-layouts: 1.27 us -> none  [per_device(): enc_gain.reshape(1, -1)]
where the time goes in v2:
time: 92.7 us; the launch traced here: 90.9 us
  Pallas kernels  89.3 us (96%)
  local copies, waits for them, and re-layouts  1.67 us (2%)
    pallas_call x1, Pallas kernels, per_device(): pl.pallas_call(kernel, out_shape=jax.ShapeDtypeStruct((256, 512), BF), in...  89.3 us

profile of v2, /device:TPU:8, one launch (start us, length us, event | category | flops | bytes accessed | tf_op | source)
XLA Modules:
  0.0 90.9 jit_solution(7936157016211143856)
XLA Ops:
  0.0 89.3 %layer.1 = bf16[256,512]{1,0:T(8,128)(2,1)} custom-call(bf16[256,512]{1,0:T(8,128)(2,1)} %hid.1, bf16[4,256,896]{2,1,0:T(8,128)(2,1)} %nb.1, f32[896]{0:T(1024)} %eg.1, bf16[448,896]{1,0:T(8,128)(2,1)} %bitcast.2, bf16[448,896]{1,0:T(8,128)(2,1)} %w2.1, bf16[896,512]{1,0:T(8,128)(2,1)} %wk.1, bf16[896,512]{1,0:T(8,128)(2,1)} %wv.1, f32[8,1,512]{2,1,0:T(1,128)} %bitcast.3, ...), custom_call_target="tpu_custom_call" | custom-call | tf_op jit(solution)/shard_map/layer/pallas_call | solution.py:481
  89.3 1.7 %copy.12 = bf16[256,512]{1,0:T(8,128)(2,1)} copy(bf16[256,512]{1,0:T(8,128)(2,1)} %layer.1) | data formatting | bytes 524288
